TPU v7x, 512 devices: a whole 4x8x8 slice. The times are simulated.
512 devices in a mesh: band: 32 (over y_hi, z, core), ga: 16 (over y_lo, x).
Axes of the slice: x: 4, y: 8 (y_hi: 2, y_lo: 4; y = y_hi * 4 + y_lo), z: 8, core: 2. Of those that a mesh axis runs over, the one named last changes fastest.
Arguments:
- valence_pairs: bfloat16 [1024, 10240], P(None, 'band'), may hold values from -6 to 6
- screened: bfloat16 [10240, 10240], P('band', 'ga'), may hold values from -0.0625 to 0.0625
- conduction_pairs: bfloat16 [65536, 10240], P('band', 'ga'), may hold values from -0.0625 to 0.0625
- window_mask: int32 [8, 512], P(None, 'band'), may hold values 0 or 1
Outputs:
- direct_kernel: bfloat16 [1024, 65536], P('ga', 'band')
All inputs are finite; a program needn't handle non-finite values. No bound on the sum of `window_mask` on one device may be relied on, other than what follows from the above.
Results may differ from a plain program's by a relative error of at most 0.017.
Values may be sent and summed in bfloat16 or wider, within the bound.
A program may use at most 64 MiB of HBM per device.

v0:
```python
import jax
import jax.numpy as jnp
from jax import lax
from jax.sharding import Mesh
from jax.sharding import PartitionSpec as P

BAND = ("band_0", "band_1", "band_2")


def split_up(value, dim, length):
    lengths = value.shape
    parts = value.reshape(*lengths[:dim], length, lengths[dim] // length, *lengths[dim + 1 :])
    return jnp.moveaxis(parts, dim, 0)


def sent_and_summed(value, axis, dim):
    parts = split_up(value, dim, lax.axis_size(axis))
    arrived = lax.all_to_all(parts, axis, split_axis=0, concat_axis=0, tiled=True)
    return arrived.sum(axis=0)


def summed_rows(value, axes, dim):
    far, near = axes
    own = sent_and_summed(split_up(value, dim, lax.axis_size(far)), near, dim + 1)
    return jnp.sum(lax.all_to_all(own, far, 0, 0, tiled=True), axis=0)


def rows_for(lines, length):
    spare = -lines.shape[0] % length
    if not spare:
        return lines
    return jnp.concatenate([lines, jnp.zeros((spare, *lines.shape[1:]), lines.dtype)])


def from_everyone(value, axis):
    length = lax.axis_size(axis)
    return lax.all_to_all(
        jnp.broadcast_to(value[None], (length, *value.shape)), axis, 0, 0, tiled=True
    )


def in_order(parts, dim):
    lengths = list(parts.shape[1:])
    lengths[dim] *= parts.shape[0]
    return jnp.moveaxis(parts, 0, dim).reshape(lengths)


def gathered_by_axis(value, axes, dim):
    far, near = axes
    first = from_everyone(value, far)
    parts = jnp.swapaxes(from_everyone(first, near), 0, 1)
    return in_order(parts.reshape(-1, *value.shape), dim)


def nested_sum(value, axes):
    lines = value.reshape(-1, value.shape[-1])
    own = summed_rows(rows_for(lines, lax.axis_size(axes[0]) * lax.axis_size(axes[1])), axes, 0)
    whole = gathered_by_axis(own, axes, 0)
    return whole[: len(lines)].reshape(value.shape)


def tile_product(segment, columns):
    return lax.dot_general(
        segment, columns, (((1,), (1,)), ((), ())), preferred_element_type=jnp.float32
    )


def local(valence_pairs, screened, conduction_pairs, window_mask):
    blocks_here = window_mask.astype(jnp.float32)
    block_count = conduction_pairs.shape[0] // 128
    partial_value = jnp.dot(valence_pairs, screened, preferred_element_type=jnp.float32)
    summed = nested_sum(partial_value, (("band_0", "band_1"), "band_2")).astype(jnp.bfloat16)
    row_count = summed.shape[0]
    row_block = jnp.arange(row_count, dtype=jnp.int32) // 128
    selector = (
        row_block[:, None] == jnp.arange(blocks_here.shape[0], dtype=jnp.int32)[None, :]
    ).astype(jnp.float32)
    weights = jnp.dot(selector, blocks_here)
    product = tile_product(summed, conduction_pairs)
    shaped = product.reshape(row_count, block_count, 128) * weights[:, :, None]
    kernel = shaped.reshape(row_count, block_count * 128)
    return lax.psum_scatter(kernel.astype(jnp.bfloat16), "ga", scatter_dimension=0, tiled=True)


def solution(mesh):
    torus = Mesh(
        mesh.devices.reshape(2, 8, 2, mesh.shape["ga"]), ("band_0", "band_1", "band_2", "ga")
    )
    return jax.shard_map(
        local,
        mesh=torus,
        in_specs=(P(None, BAND), P(BAND, "ga"), P(BAND, "ga"), P(None, BAND)),
        out_specs=P("ga", BAND),
        check_vma=False,
    )
```

profile of v0, /device:TPU:64, one launch (start us, length us, event | category | flops | bytes accessed | tf_op | source)
XLA Modules:
  0.0 218.3 jit_solution(1656222285066571129)
XLA Ops:
  6.5 0.0 copy-start
  6.5 2.3 %fusion.6 = f32[1024,640]{1,0:T(8,128)S(1)} fusion(bf16[1024,320]{0,1:T(8,128)(2,1)} %param.4, bf16[320,640]{1,0:T(8,128)(2,1)} %param.5), kind=kOutput, calls=%fused_computation.14 | convolution fusion | flops 419430400 | bytes 3686400 | tf_op jit(solution)/shard_map/dot_general | solution.py:71
  8.9 0.2 copy.13
  9.1 6.8 %all_to_all.20 = f32[2,16,32,640]{3,2,1,0:T(8,128)} all-to-all(f32[2,16,32,640]{3,2,1,0:T(8,128)S(1)} %bitcast.17), channel_id=1, replica_groups=mesh['band_0'=2,'band_1'=8,'band_2'=2,'ga'=16] {'band_2'}, dimensions={0} | all-to-all | bytes 5242880 | tf_op jit(solution)/shard_map/all_to_all | solution.py:18
  15.8 3.1 %reduce_sum.18 = f32[16,32,640]{2,1,0:T(8,128)} reduce(f32[2,16,32,640]{3,2,1,0:T(8,128)} %all_to_all.20, f32[]{:T(128)} %constant.14.clone.1), dimensions={0}, to_apply=%region_0.0 | reduce | flops 327680 | bytes 3932164 | tf_op jit(solution)/shard_map/reduce_sum | solution.py:19
  19.0 0.0 copy-start.1
  19.0 48.1 %all_to_all.21 = f32[16,32,640]{2,1,0:T(8,128)} all-to-all(f32[16,32,640]{2,1,0:T(8,128)} %reduce_sum.18), channel_id=1, replica_groups=mesh['band_0'=2,'band_1'=8,'band_2'=2,'ga'=16] {'band_0','band_1'}, dimensions={0} | all-to-all | bytes 2621440 | tf_op jit(solution)/shard_map/all_to_all | solution.py:25
  67.0 1.4 reduce_sum.19
  68.4 0.9 broadcast_in_dim.4
  69.3 9.1 %all-to-all-start.2 = ((bf16[16,32,640]{2,1,0:T(8,128)(2,1)}), bf16[16,32,640]{2,1,0:T(8,128)(2,1)S(1)}, u32[]{:S(2)}, u32[]{:S(2)}) async-start(bf16[16,32,640]{2,1,0:T(8,128)(2,1)} %broadcast_in_dim.4), calls=%async_computation.2 | async-start | bytes 1310720 | tf_op jit(solution)/shard_map/all_to_all | solution.py:37
  78.4 0.0 reduce-scatter.2.cloned.1.call-start
  78.5 0.0 copy-done.1
  78.5 0.3 fusion
  78.8 19.6 %all-to-all-done.2 = bf16[16,32,640]{2,1,0:T(8,128)(2,1)S(1)} async-done(((bf16[16,32,640]{2,1,0:T(8,128)(2,1)}), bf16[16,32,640]{2,1,0:T(8,128)(2,1)S(1)}, u32[]{:S(2)}, u32[]{:S(2)}) %all-to-all-start.2) | async-done | bytes 655392 | tf_op jit(solution)/shard_map/all_to_all | solution.py:37
  98.5 0.1 broadcast_in_dim.5
  98.6 4.8 %all_to_all.22 = bf16[2,16,32,640]{3,2,1,0:T(8,128)(2,1)S(1)} all-to-all(bf16[2,16,32,640]{3,2,1,0:T(8,128)(2,1)S(1)} %broadcast_in_dim.5), channel_id=1, replica_groups=mesh['band_0'=2,'band_1'=8,'band_2'=2,'ga'=16] {'band_2'}, dimensions={0} | all-to-all | bytes 2621440 | tf_op jit(solution)/shard_map/all_to_all | solution.py:37
  103.4 0.2 copy.10
  103.6 0.0 copy-done
  103.6 5.0 %multiply_convert_fusion = bf16[1024,16,128]{0,2,1:T(8,128)(2,1)} fusion(f32[1024,16]{0,1:T(8,128)S(1)} %fusion, bf16[1024,640,1]{1,0,2:T(8,128)(2,1)S(1)} %bitcast.21, bf16[16,128,640]{2,1,0:T(8,128)(2,1)S(1)} %bitcast.16), kind=kOutput, calls=%fused_computation | convolution fusion | flops 2688548864 | bytes 8192000 | tf_op jit(solution)/shard_map/dot_general | solution.py:63
  108.6 6.5 %copy.11 = bf16[1024,2048]{1,0:T(8,128)(2,1)} copy(bf16[1024,2048]{0,1:T(8,128)(2,1)} %bitcast.20) | data formatting | bytes 8388608 | tf_op jit(solution)/shard_map/convert_element_type | solution.py:82
  115.1 0.0 reduce-scatter.2.cloned.1.call-update
  115.1 96.4 %reduce-scatter.2.cloned.1.call-done = bf16[64,2048]{1,0:T(8,128)(2,1)} async-done(((bf16[1024,2048]{1,0:T(8,128)(2,1)}), bf16[64,2048]{1,0:T(8,128)(2,1)}) %reduce-scatter.2.cloned.1.call-update) | async-done | bytes 262160 | tf_op jit(solution)/shard_map/reduce_scatter | solution.py:82
  (1 shorter events, 0.0 us)
Async XLA Ops:
  6.5 97.0 %copy-start = (bf16[2048,640]{1,0:T(8,128)(2,1)S(1)}, bf16[2048,640]{1,0:T(8,128)(2,1)}, u32[]{:S(2)}) copy-start(bf16[2048,640]{1,0:T(8,128)(2,1)} %param.6) | copy-start | bytes 7864324
  19.0 59.5 %copy-start.1 = (s32[8,16]{1,0:T(8,128)S(1)}, s32[8,16]{1,0:T(8,128)}, u32[]{:S(2)}) copy-start(s32[8,16]{1,0:T(8,128)} %param.7) | copy-start | bytes 1540
  69.3 29.2 %all-to-all-start.2 = ((bf16[16,32,640]{2,1,0:T(8,128)(2,1)}), bf16[16,32,640]{2,1,0:T(8,128)(2,1)S(1)}, u32[]{:S(2)}, u32[]{:S(2)}) async-start(bf16[16,32,640]{2,1,0:T(8,128)(2,1)} %broadcast_in_dim.4), calls=%async_computation.2 | async-start | bytes 1310720 | tf_op jit(solution)/shard_map/all_to_all | solution.py:37
  78.4 133.1 %reduce-scatter.2.cloned.1.call-start = ((), (), s32[]{:S(2)}) async-start(), calls=%async_computation.5 | async-start | bytes 4456448 | tf_op jit(solution)/shard_map/reduce_scatter | solution.py:82
Sparse Core Ops, SparseCore 0:
  115.3 96.1 reduce-scatter.1
where the time goes:
time: 219 us; the launch traced here: 218 us
  waiting for transfers between devices  116 us (53%)
  blocking collectives  59.6 us (27%)
  between operations  13.5 us (6%)
  starting transfers between devices  9.16 us (4%)
  local copies, waits for them, and re-layouts  7.9 us (4%)
  matrix products  7.66 us (3%)
  other arithmetic  4.52 us (2%)
    reduce_scatter x1, waiting for transfers between devices, local(): lax.psum_scatter(kernel.astype(jnp.bfloat16), 'ga', scatter_dimension=0,...  96.4 us
    all_to_all x1, blocking collectives, summed_rows(): return jnp.sum(lax.all_to_all(own, far, 0, 0, tiled=True), axis=0)  48.1 us
    all_to_all x1, waiting for transfers between devices, from_everyone(): lax.all_to_all(jnp.broadcast_to(value[None], (length, *value.shape)), axi...  19.6 us
    all_to_all x1, starting transfers between devices, from_everyone(): lax.all_to_all(jnp.broadcast_to(value[None], (length, *value.shape)), axi...  9.13 us
    all_to_all x1, blocking collectives, sent_and_summed(): lax.all_to_all(parts, axis, split_axis=0, concat_axis=0, tiled=True)  6.76 us
    convert_element_type x1, local copies, waits for them, and re-layouts, local(): kernel.astype(jnp.bfloat16)  6.52 us
    dot_general x1, matrix products, tile_product(): lax.dot_general(segment, columns, (((1,), (1,)), ((), ())), preferred_ele...  5.01 us
    all_to_all x1, blocking collectives, from_everyone(): lax.all_to_all(jnp.broadcast_to(value[None], (length, *value.shape)), axi...  4.79 us
  transfers between devices with their start and end apart: 2, of which 2 were waited for; matrix products, arithmetic and copies ran while one was open for 0% of the time, Pallas kernels for 0%

commit v1 on v0

v1 whole, which is shorter than its diff:
```python
import jax
import jax.numpy as jnp
from jax import lax
from jax.experimental import pallas as pl
from jax.experimental.pallas import tpu as pltpu
from jax.sharding import Mesh
from jax.sharding import PartitionSpec as P

MESH = pl.DeviceIdType.MESH
BAND = ("yh", "z", "c")
GA = ("y", "x")
F32 = jnp.float32
BF16 = jnp.bfloat16

NZ, NY, NX = 8, 4, 4
NJ = 4
RW = 16
SPLIT = 1536
HOPS = (4, 3, 5, 2, 6, 1, 7)


def schedule():
    start = (0.0, 3.0, 13.0, 20.0)
    first = 25.0
    events = []
    for j in range(NJ):
        t = start[j]
        for name, dt in (("S0", 0), ("S1", 2.5), ("S2", 10), ("S3", 15), ("S4", 23)):
            events.append((t + dt, name, j))
        t = first + 7.4 * j
        for name, dt in (
            ("PB", 0), ("BY0", 0.1), ("PA", 0.2), ("AX1", 0.3),
            ("AX2", 5), ("BY1", 5.1), ("AX3", 9), ("AY0", 9.1), ("BY2", 9.2),
            ("AY1", 13), ("BY3", 13.1), ("BX1", 13.2), ("AY2", 16), ("BX2", 16.1),
            ("AY3", 19), ("AF", 19.1), ("BX3", 19.2),
        ):
            events.append((t + dt, name, j))
    events.sort(key=lambda e: e[0])
    return [(name, j) for _, name, j in events]


def kernel(v_hbm, w_hbm, c_hbm, mask, out, v, w, cc, core_s, core_r, own, zs, zr, ysum, ys, yr,
           sv, pb, rb, rb16, ra, xra, xsa, xrb, xsb, yra, ysa, yrb, ysb,
           in_sem, one_s, one_r, xa_s, xa_r, xb_s, xb_r, y_s, y_r):
    yh, z, c = lax.axis_index("yh"), lax.axis_index("z"), lax.axis_index("c")
    y, x = lax.axis_index("y"), lax.axis_index("x")
    xp, xf, xm = lax.rem(x + 1, NX), lax.rem(x + 2, NX), lax.rem(x + 3, NX)

    loads = [
        pltpu.make_async_copy(v_hbm, v, in_sem.at[0]),
        pltpu.make_async_copy(w_hbm, w, in_sem.at[1]),
        pltpu.make_async_copy(c_hbm, cc, in_sem.at[2]),
    ]
    for load in loads:
        load.start()

    def at_z(k):
        return (yh, lax.rem(z + k, NZ), c, y, x)

    partner = (yh, z, 1 - c, y, x)
    far = (1 - yh, z, c, y, x)
    right, left = (yh, z, c, y, xp), (yh, z, c, y, xm)
    up, down = (yh, z, c, y + 1, x), (yh, z, c, y - 1, x)

    barrier = pltpu.get_barrier_semaphore()

    def greet(device):
        pl.semaphore_signal(barrier, inc=1, device_id=device, device_id_type=MESH)

    for k in HOPS:
        greet(at_z(k))
    for device in (far, right, left, partner):
        greet(device)
    pl.when(y < NY - 1)(lambda: greet(up))
    pl.when(y > 0)(lambda: greet(down))

    def send(src, dst, s_sem, r_sem, device):
        pltpu.make_async_remote_copy(
            src_ref=src, dst_ref=dst, send_sem=s_sem, recv_sem=r_sem,
            device_id=device, device_id_type=MESH,
        ).start()

    def arrived(ref, sem):
        pltpu.make_async_copy(ref, ref, sem).wait()

    def partial(half, j):
        rows = v[pl.ds(half * 8, 8), j * RW:(j + 1) * RW, :].reshape(128, -1)
        return jnp.dot(rows, w[...], preferred_element_type=F32).reshape(8, RW, -1)

    def S0(j):
        core_s[j] = partial(1 - c, j).astype(BF16)
        if j == 0:
            pl.semaphore_wait(
                barrier, 11 + (y > 0).astype(jnp.int32) + (y < NY - 1).astype(jnp.int32)
            )
        send(core_s.at[j], core_r.at[j], one_s.at[j, 0], one_r.at[j, 0], partner)
        own[j] = partial(c, j)

    def S1(j):
        arrived(core_r.at[j], one_r.at[j, 0])
        total = own[j] + core_r[j].astype(F32)
        own[j] = total
        zs[j] = total.astype(BF16)
        for k in HOPS:
            send(zs.at[j, lax.rem(z + k, NZ)], zr.at[j, k - 1],
                 one_s.at[j, 1], one_r.at[j, 1], at_z(k))

    def S2(j):
        arrived(zr.at[j], one_r.at[j, 1])
        total = own[j, z]
        for k in range(NZ - 1):
            total = total + zr[j, k].astype(F32)
        ysum[j] = total
        ys[j] = total.astype(BF16)
        send(ys.at[j], yr.at[j], one_s.at[j, 2], one_r.at[j, 2], far)

    def S3(j):
        arrived(yr.at[j], one_r.at[j, 2])
        mine = c * NZ + z
        sv[j, mine] = (ysum[j] + yr[j].astype(F32)).astype(BF16)
        for k in HOPS:
            send(sv.at[j, mine], sv.at[j, mine], one_s.at[j, 3], one_r.at[j, 3], at_z(k))

    def S4(j):
        arrived(zr.at[j], one_r.at[j, 3])
        half = sv.at[j, pl.ds(c * NZ, NZ)]
        send(half, half, one_s.at[j, 4], one_r.at[j, 4], partner)

    def product(j, first, count):
        rows = sv[j].reshape(256, -1)

        def tile(t, carry):
            at = pl.multiple_of(first + t * 256, 256)
            block = lax.dot_general(
                rows, cc[pl.ds(at, 256), :], (((1,), (1,)), ((), ())), preferred_element_type=F32
            )
            pb[j, :, :, :, pl.ds(at, 256)] = block.astype(BF16).reshape(NY, NX, RW, 256)
            return carry

        lax.fori_loop(0, count // 256, tile, 0)

    width = out.shape[1]
    tail = width - SPLIT
    b_cols = pl.ds(SPLIT, tail)

    def PB(j):
        arrived(sv.at[j, pl.ds(0, NZ)], one_r.at[j, 4])
        if j == 0:
            loads[2].wait()
        product(j, SPLIT, tail)

    def PA(j):
        product(j, 0, SPLIT)

    half_a, half_b = SPLIT // 2, tail // 2

    def a_part(j, i, half):
        return pb.at[j, :, i, :, pl.ds(half * half_a, half_a)]

    def b_part(j, i, half):
        return rb16.at[j, i, :, pl.ds(half * half_b, half_b)]

    def x_first(j, part, got, s_sem, r_sem):
        send(part(j, xf, 0), got.at[j, 0], s_sem.at[j, 0], r_sem.at[j, 0], right)
        send(part(j, xf, 1), got.at[j, 3], s_sem.at[j, 3], r_sem.at[j, 3], left)
        send(part(j, xp, 1), got.at[j, 1], s_sem.at[j, 1], r_sem.at[j, 1], right)
        send(part(j, xm, 0), got.at[j, 4], s_sem.at[j, 4], r_sem.at[j, 4], left)

    def x_second(j, part, got, out_buf, s_sem, r_sem):
        for slot, i, half, device in ((0, xp, 0, right), (3, xm, 1, left)):
            arrived(got.at[j, slot], r_sem.at[j, slot])
            mine = part(j, i, half)[...]
            out_buf[j, slot // 3] = (mine.astype(F32) + got[j, slot].astype(F32)).astype(BF16)
            send(out_buf.at[j, slot // 3], got.at[j, slot + 2],
                 s_sem.at[j, slot + 2], r_sem.at[j, slot + 2], device)

    def x_third(j, got, r_sem, half):
        a, b = ((2, 4), (1, 5))[half]
        arrived(got.at[j, a], r_sem.at[j, a])
        arrived(got.at[j, b], r_sem.at[j, b])
        return got[j, a].astype(F32) + got[j, b].astype(F32)

    def AX1(j):
        x_first(j, a_part, xra, xa_s, xa_r)

    def AX2(j):
        x_second(j, a_part, xra, xsa, xa_s, xa_r)

    def AX3(j):
        for half in (0, 1):
            ra[j, :, :, half * half_a:(half + 1) * half_a] = (
                x_third(j, xra, xa_r, half) + a_part(j, x, half)[...].astype(F32)
            )

    def BX1(j):
        rb16[j] = rb[j].astype(BF16)
        x_first(j, b_part, xrb, xb_s, xb_r)

    def BX2(j):
        x_second(j, b_part, xrb, xsb, xb_s, xb_r)

    row_block = (y * NX + x) // 2

    def finish(j, first, value):
        for t in range(value.shape[1] // 128):
            live = mask[row_block, first // 128 + t].astype(F32)
            out[j * RW:(j + 1) * RW, first + t * 128:first + (t + 1) * 128] = (
                value[:, t * 128:(t + 1) * 128] * live
            ).astype(BF16)

    def BX3(j):
        for half in (0, 1):
            value = x_third(j, xrb, xb_r, half) + rb[j, x, :, half * half_b:(half + 1) * half_b]
            finish(j, SPLIT + half * half_b, value)

    def AF(j):
        finish(j, 0, ra[j, y])

    def y_step(j, h, p):
        got, buf = (yra, ysa) if p == 0 else (yrb, ysb)

        def own_blocks(lo, hi):
            if p == 0:
                return ra[j, lo:hi]
            return pb[j, lo:hi, :, :, SPLIT:].astype(F32)

        def one_way(d):
            lo, hi = (h + 1, NY) if d == 0 else (0, NY - 1 - h)
            keep = h if d == 0 else NY - 1 - h
            if h > 0:
                block = got.at[j, d, keep:NY] if d == 0 else got.at[j, d, 0:keep + 1]
                arrived(block, y_r.at[j, p, d])
                if p == 0:
                    ra[j, keep] = ra[j, keep] + got[j, d, keep].astype(F32)
                else:
                    rb[j] = rb[j] + got[j, d, keep].astype(F32)
            if h < NY - 1:
                if p == 1 and h == 0:
                    src = pb.at[j, lo:hi, :, :, b_cols]
                else:
                    value = own_blocks(lo, hi)
                    if h > 0:
                        value = value + got[j, d, lo:hi].astype(F32)
                    buf[j, d, lo:hi] = value.astype(BF16)
                    src = buf.at[j, d, lo:hi]
                send(src, got.at[j, d, lo:hi], y_s.at[j, p], y_r.at[j, p, d], up if d == 0 else down)

        if p == 1 and h == 0:
            rb[j] = pb[j, y, :, :, SPLIT:].astype(F32)
        pl.when(y == h)(lambda: one_way(0))
        pl.when(y == NY - 1 - h)(lambda: one_way(1))

    steps = dict(S0=S0, S1=S1, S2=S2, S3=S3, S4=S4, PB=PB, PA=PA, AX1=AX1, AX2=AX2, AX3=AX3,
                 BX1=BX1, BX2=BX2, BX3=BX3, AF=AF)
    for h in range(NY):
        steps[f"AY{h}"] = lambda j, h=h: y_step(j, h, 0)
        steps[f"BY{h}"] = lambda j, h=h: y_step(j, h, 1)

    loads[0].wait()
    loads[1].wait()
    for name, j in schedule():
        steps[name](j)

    for j in range(NJ):
        arrived(core_s.at[j], one_s.at[j, 0])
        arrived(zr.at[j], one_s.at[j, 1])
        arrived(ys.at[j], one_s.at[j, 2])
        arrived(zr.at[j], one_s.at[j, 3])
        arrived(sv.at[j, pl.ds(0, NZ)], one_s.at[j, 4])
        for slot in range(6):
            arrived(xra.at[j, slot], xa_s.at[j, slot])
            arrived(xrb.at[j, slot], xb_s.at[j, slot])
        arrived(yra.at[j, 0, 0:3], y_s.at[j, 0])
        arrived(yrb.at[j, 0, 0:3], y_s.at[j, 1])


def local(valence_pairs, screened, conduction_pairs, window_mask):
    rows, depth = valence_pairs.shape
    inner = screened.shape[1]
    width = conduction_pairs.shape[0]
    tail = width - SPLIT
    v3 = valence_pairs.reshape(NY * NX, rows // (NY * NX), depth)
    vmem, dma = pltpu.VMEM, pltpu.SemaphoreType.DMA
    any_space = pl.BlockSpec(memory_space=pl.ANY)
    scratch = [
        vmem(v3.shape, BF16), vmem(screened.shape, BF16), vmem(conduction_pairs.shape, BF16),
        vmem((NJ, NZ, RW, inner), BF16), vmem((NJ, NZ, RW, inner), BF16),
        vmem((NJ, NZ, RW, inner), F32),
        vmem((NJ, NZ, RW, inner), BF16), vmem((NJ, NZ - 1, RW, inner), BF16),
        vmem((NJ, RW, inner), F32), vmem((NJ, RW, inner), BF16), vmem((NJ, RW, inner), BF16),
        vmem((NJ, 2 * NZ, RW, inner), BF16),
        vmem((NJ, NY, NX, RW, width), BF16),
        vmem((NJ, NX, RW, tail), F32), vmem((NJ, NX, RW, tail), BF16),
        vmem((NJ, NY, RW, SPLIT), F32),
        vmem((NJ, 6, NY, RW, SPLIT // 2), BF16), vmem((NJ, 2, NY, RW, SPLIT // 2), BF16),
        vmem((NJ, 6, RW, tail // 2), BF16), vmem((NJ, 2, RW, tail // 2), BF16),
        vmem((NJ, 2, NY, RW, SPLIT), BF16), vmem((NJ, 2, NY, RW, SPLIT), BF16),
        vmem((NJ, 2, NY, NX, RW, tail), BF16), vmem((NJ, 2, NY, NX, RW, tail), BF16),
        dma((3,)), dma((NJ, 5)), dma((NJ, 5)),
        dma((NJ, 6)), dma((NJ, 6)), dma((NJ, 6)), dma((NJ, 6)),
        dma((NJ, 2)), dma((NJ, 2, 2)),
    ]
    return pl.pallas_call(
        kernel,
        out_shape=jax.ShapeDtypeStruct((rows // (NY * NX), width), BF16),
        in_specs=[any_space, any_space, any_space, pl.BlockSpec(memory_space=pltpu.SMEM)],
        out_specs=pl.BlockSpec(memory_space=pltpu.VMEM),
        scratch_shapes=scratch,
        compiler_params=pltpu.CompilerParams(
            collective_id=0, has_side_effects=True, vmem_limit_bytes=56 * 1024 * 1024
        ),
        name="window",
    )(v3, screened, conduction_pairs, window_mask)


def solution(mesh):
    torus = Mesh(mesh.devices.reshape(2, NZ, 2, NY, NX), BAND + GA)
    return jax.shard_map(
        local,
        mesh=torus,
        in_specs=(P(None, BAND), P(BAND, GA), P(BAND, GA), P(None, BAND)),
        out_specs=P(GA, BAND),
        check_vma=False,
    )
```

time: 219 us -> 93.7 us (0.43)
  the two profiles are of different devices: /device:TPU:64 before, /device:TPU:2 now
where the time goes in v1:
time: 93.7 us; the launch traced here: 93.5 us
  Pallas kernels  89.6 us (96%)
  local copies, waits for them, and re-layouts  3.91 us (4%)
    pallas_call x1, Pallas kernels, local(): pl.pallas_call(kernel, out_shape=jax.ShapeDtypeStruct((rows // (NY * NX),...  89.6 us
    unnamed x2, local copies, waits for them, and re-layouts  3.91 us

profile of v1, /device:TPU:2, one launch (start us, length us, event | category | flops | bytes accessed | tf_op | source)
XLA Modules:
  0.0 93.5 jit_solution(11068403561478935193)
XLA Ops:
  0.0 2.2 %copy.5 = bf16[1024,320]{1,0:T(8,128)(2,1)} copy(bf16[1024,320]{0,1:T(8,128)(2,1)} %param.4) | data formatting | bytes 1310720 | tf_op args[0]
  2.2 89.6 %window.1 = bf16[64,2048]{1,0:T(8,128)(2,1)} custom-call(bf16[16,64,320]{2,1,0:T(8,128)(2,1)} %bitcast.1, bf16[320,640]{1,0:T(8,128)(2,1)} %w_hbm.1, bf16[2048,640]{1,0:T(8,128)(2,1)} %c_hbm.1, s32[8,16]{1,0:T(8,128)} %mask.1), custom_call_target="tpu_custom_call" | custom-call | tf_op jit(solution)/shard_map/window/pallas_call | solution.py:303
  91.8 1.7 %copy.7 = bf16[64,2048]{1,0:T(8,128)(2,1)} copy(bf16[64,2048]{1,0:T(8,128)(2,1)} %window.1) | data formatting | bytes 524288

commit v2 on v1

v2 whole, which is shorter than its diff:
```python
import jax
import jax.numpy as jnp
from jax import lax
from jax.experimental import pallas as pl
from jax.experimental.pallas import tpu as pltpu
from jax.sharding import Mesh
from jax.sharding import PartitionSpec as P

MESH = pl.DeviceIdType.MESH
BAND = ("yh", "z", "c")
GA = ("y", "x")
F32 = jnp.float32
BF16 = jnp.bfloat16

NZ, NY, NX = 8, 4, 4
NJ = 4
RW = 16
SPLIT = 1792
HOPS = (4, 3, 5, 2, 6, 1, 7)
UNITS = (((0, 1024), (1024, 768)),) * NJ


def schedule():
    times = {
        "S1": (2.5, 2.6, 11.1, 20.2), "S2": (11, 15.3, 20.3, 30),
        "S3": (15.8, 20.1, 25.2, 35), "S4": (21.7, 26.5, 31.5, 41),
    }
    events = [(t, name, j, 0) for name, row in times.items() for j, t in enumerate(row)]
    for j in range(NJ):
        t = 23 + 7.7 * j
        for dt, name, u in (
            (0, "PB", 0), (0.1, "XF", 0), (0.2, "XD", 0), (0.3, "XF", 1),
            (5.0, "X2", 0), (5.1, "XD", 1), (7.2, "X2", 1), (7.3, "BS", 0), (9.5, "X3", 0), (12, "X3", 1),
            (12.1, "B2", 0), (16, "B3", 0), (17, "YF", 0), (19, "YF", 1),
        ):
            events.append((t + dt, name, j, u))
    events.sort(key=lambda e: e[0])
    return [e[1:] for e in events]


def kernel(v_hbm, w_hbm, c_hbm, mask, out, v, w, cc, core_s, core_r, own, zs, zr, ysum, ys, yr,
           sv, pb, far_r, dir_r, mrg_s, mrg_r, ya_s, ya_r, yb_r, rb, rb16, bfar, bdir, bms, bmr,
           in_sem, one_s, one_r, xa_s, xa_r, ya_ss, ya_rs, yb_ss, yb_rs, xb_s, xb_r):
    yh, z, c = lax.axis_index("yh"), lax.axis_index("z"), lax.axis_index("c")
    y, x = lax.axis_index("y"), lax.axis_index("x")
    xp, xf, xm = lax.rem(x + 1, NX), lax.rem(x + 2, NX), lax.rem(x + 3, NX)

    loads = [
        pltpu.make_async_copy(v_hbm, v, in_sem.at[0]),
        pltpu.make_async_copy(w_hbm, w, in_sem.at[1]),
        pltpu.make_async_copy(c_hbm, cc, in_sem.at[2]),
    ]
    loads[0].start()
    loads[1].start()

    def at_z(k):
        return (yh, lax.rem(z + k, NZ), c, y, x)

    def at_y(k):
        return (yh, z, c, lax.rem(y + k, NY), x)

    partner = (yh, z, 1 - c, y, x)
    far = (1 - yh, z, c, y, x)
    right, left = (yh, z, c, y, xp), (yh, z, c, y, xm)

    barrier = pltpu.get_barrier_semaphore()
    peers = [at_z(k) for k in HOPS] + [far] + [at_y(k) for k in (1, 2, 3)] + [right, left, partner]
    for device in peers:
        pl.semaphore_signal(barrier, inc=1, device_id=device, device_id_type=MESH)

    def send(src, dst, s_sem, r_sem, device):
        pltpu.make_async_remote_copy(
            src_ref=src, dst_ref=dst, send_sem=s_sem, recv_sem=r_sem,
            device_id=device, device_id_type=MESH,
        ).start()

    def arrived(ref, sem):
        pltpu.make_async_copy(ref, ref, sem).wait()

    def partial(half, t):
        lanes = pl.ds(pl.multiple_of(half * 512 + t * 128, 128), 128)
        value = lax.dot_general(
            v[:, lanes], w[...], (((0,), (0,)), ((), ())), preferred_element_type=F32
        )
        return value.reshape(2, NJ, RW, -1)

    loads[0].wait()
    loads[1].wait()
    loads[2].start()

    def for_partner(t, carry):
        value = partial(1 - c, t).astype(BF16)
        for j in range(NJ):
            core_s[j, pl.ds(2 * t, 2)] = value[:, j]
        return carry

    lax.fori_loop(0, 4, for_partner, 0)
    pl.semaphore_wait(barrier, len(peers))
    for j in range(NJ):
        send(core_s.at[j], core_r.at[j], one_s.at[j, 0], one_r.at[j, 0], partner)

    def for_self(t, carry):
        value = partial(c, t)
        for j in range(NJ):
            own[j, pl.ds(2 * t, 2)] = value[:, j]
        return carry

    lax.fori_loop(0, 4, for_self, 0)

    def S1(j, u):
        arrived(core_r.at[j], one_r.at[j, 0])
        total = own[j] + core_r[j].astype(F32)
        own[j] = total
        zs[j] = total.astype(BF16)
        for k in HOPS:
            send(zs.at[j, lax.rem(z + k, NZ)], zr.at[j, k - 1],
                 one_s.at[j, 1], one_r.at[j, 1], at_z(k))

    def S2(j, u):
        arrived(zr.at[j], one_r.at[j, 1])
        total = own[j, z]
        for k in range(NZ - 1):
            total = total + zr[j, k].astype(F32)
        ysum[j] = total
        ys[j] = total.astype(BF16)
        send(ys.at[j], yr.at[j], one_s.at[j, 2], one_r.at[j, 2], far)

    def S3(j, u):
        arrived(yr.at[j], one_r.at[j, 2])
        mine = c * NZ + z
        sv[j, mine] = (ysum[j] + yr[j].astype(F32)).astype(BF16)
        for k in HOPS:
            send(sv.at[j, mine], sv.at[j, mine], one_s.at[j, 3], one_r.at[j, 3], at_z(k))

    def S4(j, u):
        arrived(zr.at[j], one_r.at[j, 3])
        half = sv.at[j, pl.ds(c * NZ, NZ)]
        send(half, half, one_s.at[j, 4], one_r.at[j, 4], partner)

    def product(j, first, count):
        rows = sv[j].reshape(256, -1)

        def tile(t, carry):
            at = pl.multiple_of(first + t * 256, 256)
            block = lax.dot_general(
                rows, cc[pl.ds(at, 256), :], (((1,), (1,)), ((), ())), preferred_element_type=F32
            )
            pb[j, :, :, :, pl.ds(at, 256)] = block.astype(BF16).reshape(NY, NX, RW, 256)
            return carry

        lax.fori_loop(0, count // 256, tile, 0)

    width = out.shape[1]
    tail = width - SPLIT
    b_cols = pl.ds(SPLIT, tail)

    def PB(j, u):
        arrived(sv.at[j, pl.ds(0, NZ)], one_r.at[j, 4])
        if j == 0:
            loads[2].wait()
        product(j, SPLIT, tail)
        for k in (3, 2, 1):
            send(pb.at[j, lax.rem(y + k, NY), :, :, b_cols], yb_r.at[j, k - 1],
                 yb_ss.at[j], yb_rs.at[j], at_y(k))

    def halves(j, u):
        lo, w_u = UNITS[j][u]
        return pl.ds(lo, w_u // 2), pl.ds(lo + w_u // 2, w_u // 2)

    def XF(j, u):
        product(j, *UNITS[j][u])
        h0, h1 = halves(j, u)
        send(pb.at[j, :, xf, :, h0], far_r.at[j, :, :, h0], xa_s.at[j, u, 0], xa_r.at[j, u, 0], right)
        send(pb.at[j, :, xf, :, h1], far_r.at[j, :, :, h1], xa_s.at[j, u, 1], xa_r.at[j, u, 1], left)

    def XD(j, u):
        h0, h1 = halves(j, u)
        send(pb.at[j, :, xp, :, h1], dir_r.at[j, :, :, h1], xa_s.at[j, u, 2], xa_r.at[j, u, 2], right)
        send(pb.at[j, :, xm, :, h0], dir_r.at[j, :, :, h0], xa_s.at[j, u, 3], xa_r.at[j, u, 3], left)

    def X2(j, u):
        for i, (h, to, device) in enumerate(zip(halves(j, u), (xp, xm), (right, left))):
            arrived(far_r.at[j, :, :, h], xa_r.at[j, u, i])
            mrg_s[j, :, :, h] = (pb[j, :, to, :, h].astype(F32) + far_r[j, :, :, h].astype(F32)).astype(BF16)
            send(mrg_s.at[j, :, :, h], mrg_r.at[j, :, :, h], xa_s.at[j, u, 4 + i], xa_r.at[j, u, 4 + i], device)

    def X3(j, u):
        h0, h1 = halves(j, u)
        arrived(dir_r.at[j, :, :, h1], xa_r.at[j, u, 2])
        arrived(dir_r.at[j, :, :, h0], xa_r.at[j, u, 3])
        arrived(mrg_r.at[j, :, :, h0], xa_r.at[j, u, 4])
        arrived(mrg_r.at[j, :, :, h1], xa_r.at[j, u, 5])
        cols = pl.ds(*UNITS[j][u])
        for k in (3, 2, 1):
            yd = lax.rem(y + k, NY)
            ya_s[j, k - 1, :, cols] = (
                pb[j, yd, x, :, cols].astype(F32) + dir_r[j, yd, :, cols].astype(F32)
                + mrg_r[j, yd, :, cols].astype(F32)
            ).astype(BF16)
            send(ya_s.at[j, k - 1, :, cols], ya_r.at[j, k - 1, :, cols],
                 ya_ss.at[j, u], ya_rs.at[j, u], at_y(k))

    row_block = (y * NX + x) // 2

    def finish(j, first, value):
        for t in range(value.shape[1] // 128):
            live = mask[row_block, first // 128 + t].astype(F32)
            out[j * RW:(j + 1) * RW, first + t * 128:first + (t + 1) * 128] = (
                value[:, t * 128:(t + 1) * 128] * live
            ).astype(BF16)

    def YF(j, u):
        lo, w_u = UNITS[j][u]
        cols = pl.ds(lo, w_u)
        arrived(ya_r.at[j, :, :, cols], ya_rs.at[j, u])
        total = (
            pb[j, y, x, :, cols].astype(F32) + dir_r[j, y, :, cols].astype(F32)
            + mrg_r[j, y, :, cols].astype(F32)
        )
        for k in range(3):
            total = total + ya_r[j, k, :, cols].astype(F32)
        finish(j, lo, total)

    b0, b1 = pl.ds(0, tail // 2), pl.ds(tail // 2, tail // 2)

    def BS(j, u):
        arrived(yb_r.at[j], yb_rs.at[j])
        total = pb[j, y, :, :, b_cols].astype(F32)
        for k in range(3):
            total = total + yb_r[j, k].astype(F32)
        rb[j] = total
        rb16[j] = total.astype(BF16)
        send(rb16.at[j, xf, :, b0], bfar.at[j, :, b0], xb_s.at[j, 0], xb_r.at[j, 0], right)
        send(rb16.at[j, xf, :, b1], bfar.at[j, :, b1], xb_s.at[j, 1], xb_r.at[j, 1], left)
        send(rb16.at[j, xp, :, b1], bdir.at[j, :, b1], xb_s.at[j, 2], xb_r.at[j, 2], right)
        send(rb16.at[j, xm, :, b0], bdir.at[j, :, b0], xb_s.at[j, 3], xb_r.at[j, 3], left)

    def B2(j, u):
        for i, (h, to, device) in enumerate(zip((b0, b1), (xp, xm), (right, left))):
            arrived(bfar.at[j, :, h], xb_r.at[j, i])
            bms[j, :, h] = (rb[j, to, :, h] + bfar[j, :, h].astype(F32)).astype(BF16)
            send(bms.at[j, :, h], bmr.at[j, :, h], xb_s.at[j, 4 + i], xb_r.at[j, 4 + i], device)

    def B3(j, u):
        arrived(bdir.at[j, :, b1], xb_r.at[j, 2])
        arrived(bdir.at[j, :, b0], xb_r.at[j, 3])
        arrived(bmr.at[j, :, b0], xb_r.at[j, 4])
        arrived(bmr.at[j, :, b1], xb_r.at[j, 5])
        finish(j, SPLIT, rb[j, x] + bdir[j].astype(F32) + bmr[j].astype(F32))

    steps = dict(S1=S1, S2=S2, S3=S3, S4=S4, PB=PB, XF=XF, XD=XD, X2=X2, X3=X3, YF=YF, BS=BS, B2=B2, B3=B3)
    for name, j, u in schedule():
        steps[name](j, u)

    for j in range(NJ):
        arrived(core_s.at[j], one_s.at[j, 0])
        arrived(zr.at[j], one_s.at[j, 1])
        arrived(ys.at[j], one_s.at[j, 2])
        arrived(zr.at[j], one_s.at[j, 3])
        arrived(sv.at[j, pl.ds(0, NZ)], one_s.at[j, 4])
        for u, (lo, w_u) in enumerate(UNITS[j]):
            for slot in range(6):
                arrived(far_r.at[j, :, :, pl.ds(lo, w_u // 2)], xa_s.at[j, u, slot])
            arrived(ya_r.at[j, :, :, pl.ds(lo, w_u)], ya_ss.at[j, u])
        arrived(yb_r.at[j], yb_ss.at[j])
        for slot in range(6):
            arrived(bfar.at[j, :, b0], xb_s.at[j, slot])


def local(valence_pairs, screened, conduction_pairs, window_mask):
    inner = screened.shape[1]
    width = conduction_pairs.shape[0]
    tail = width - SPLIT
    vt = valence_pairs.T
    vmem, dma = pltpu.VMEM, pltpu.SemaphoreType.DMA
    any_space = pl.BlockSpec(memory_space=pl.ANY)
    nu = max(len(units) for units in UNITS)
    scratch = [
        vmem(vt.shape, BF16), vmem(screened.shape, BF16), vmem(conduction_pairs.shape, BF16),
        vmem((NJ, NZ, RW, inner), BF16), vmem((NJ, NZ, RW, inner), BF16),
        vmem((NJ, NZ, RW, inner), F32),
        vmem((NJ, NZ, RW, inner), BF16), vmem((NJ, NZ - 1, RW, inner), BF16),
        vmem((NJ, RW, inner), F32), vmem((NJ, RW, inner), BF16), vmem((NJ, RW, inner), BF16),
        vmem((NJ, 2 * NZ, RW, inner), BF16),
        vmem((NJ, NY, NX, RW, width), BF16),
        vmem((NJ, NY, RW, SPLIT), BF16), vmem((NJ, NY, RW, SPLIT), BF16),
        vmem((NJ, NY, RW, SPLIT), BF16), vmem((NJ, NY, RW, SPLIT), BF16),
        vmem((NJ, NY - 1, RW, SPLIT), BF16), vmem((NJ, NY - 1, RW, SPLIT), BF16),
        vmem((NJ, NY - 1, NX, RW, tail), BF16),
        vmem((NJ, NX, RW, tail), F32), vmem((NJ, NX, RW, tail), BF16),
        vmem((NJ, RW, tail), BF16), vmem((NJ, RW, tail), BF16),
        vmem((NJ, RW, tail), BF16), vmem((NJ, RW, tail), BF16),
        dma((3,)), dma((NJ, 5)), dma((NJ, 5)),
        dma((NJ, nu, 6)), dma((NJ, nu, 6)), dma((NJ, nu)), dma((NJ, nu)), dma((NJ,)), dma((NJ,)),
        dma((NJ, 6)), dma((NJ, 6)),
    ]
    return pl.pallas_call(
        kernel,
        out_shape=jax.ShapeDtypeStruct((NJ * RW, width), BF16),
        in_specs=[any_space, any_space, any_space, pl.BlockSpec(memory_space=pltpu.SMEM)],
        out_specs=pl.BlockSpec(memory_space=pltpu.VMEM),
        scratch_shapes=scratch,
        compiler_params=pltpu.CompilerParams(
            collective_id=0, has_side_effects=True, vmem_limit_bytes=56 * 1024 * 1024
        ),
        name="window",
    )(vt, screened, conduction_pairs, window_mask)


def solution(mesh):
    torus = Mesh(mesh.devices.reshape(2, NZ, 2, NY, NX), BAND + GA)
    return jax.shard_map(
        local,
        mesh=torus,
        in_specs=(P(None, BAND), P(BAND, GA), P(BAND, GA), P(None, BAND)),
        out_specs=P(GA, BAND),
        check_vma=False,
    )
```

time: 93.7 us -> 80.4 us (0.86)
  the two profiles are of different devices: /device:TPU:2 before, /device:TPU:1 now
where the time goes in v2:
time: 80.4 us; the launch traced here: 80.2 us
  Pallas kernels  78.5 us (98%)
  local copies, waits for them, and re-layouts  1.67 us (2%)
    pallas_call x1, Pallas kernels, local(): pl.pallas_call(kernel, out_shape=jax.ShapeDtypeStruct((NJ * RW, width), B...  78.5 us
    unnamed x1, local copies, waits for them, and re-layouts  1.67 us

profile of v2, /device:TPU:1, one launch (start us, length us, event | category | flops | bytes accessed | tf_op | source)
XLA Modules:
  0.0 80.2 jit_solution(11967221590430430463)
XLA Ops:
  0.0 78.5 %window.1 = bf16[64,2048]{1,0:T(8,128)(2,1)} custom-call(bf16[320,1024]{1,0:T(8,128)(2,1)} %bitcast.1, bf16[320,640]{1,0:T(8,128)(2,1)} %w_hbm.1, bf16[2048,640]{1,0:T(8,128)(2,1)} %c_hbm.1, s32[8,16]{1,0:T(8,128)} %mask.1), custom_call_target="tpu_custom_call" | custom-call | tf_op jit(solution)/shard_map/window/pallas_call | solution.py:297
  78.5 1.7 %copy.6 = bf16[64,2048]{1,0:T(8,128)(2,1)} copy(bf16[64,2048]{1,0:T(8,128)(2,1)} %window.1) | data formatting | bytes 524288

commit v3 on v2

--- a/solution.py
+++ b/solution.py
@@ -15,27 +15,26 @@
 NZ, NY, NX = 8, 4, 4
 NJ = 4
 RW = 16
-SPLIT = 1792
 HOPS = (4, 3, 5, 2, 6, 1, 7)
-UNITS = (((0, 1024), (1024, 768)),) * NJ
+UNITS = (
+    ((0, 1024), (1024, 768)),
+    ((0, 1024), (1024, 768)),
+    ((0, 1024), (1024, 768)),
+    ((0, 1024), (1024, 768)),
+)
+SPLIT = tuple(sum(units[-1]) for units in UNITS)
+ORDER = (
+    "S100", "S120", "S110", "S200", "S220", "S300", "S210", "S320", "S130", "S400", "PB00", "XF01",
+    "XD01", "XF00", "S420", "S310", "XD00", "PB20", "XF20", "S230", "X200", "XD20", "XF21", "S410",
+    "PB10", "X220", "X300", "XD21", "X201", "S330", "XF11", "XF10", "X221", "X320", "S430", "XD10",
+    "XD11", "X301", "PB30", "XF30", "X211", "X321", "XF31", "X210", "XD30", "X230", "X311", "BS10",
+    "XD31", "X310", "BS00", "X231", "BS20", "X330", "BS30", "YF11", "YF00", "X331", "B210", "B230",
+    "B200", "YF21", "B220", "YF20", "B330", "YF01", "YF10", "B300", "B320", "YF30", "B310", "YF31",
+)
 
 
 def schedule():
-    times = {
-        "S1": (2.5, 2.6, 11.1, 20.2), "S2": (11, 15.3, 20.3, 30),
-        "S3": (15.8, 20.1, 25.2, 35), "S4": (21.7, 26.5, 31.5, 41),
-    }
-    events = [(t, name, j, 0) for name, row in times.items() for j, t in enumerate(row)]
-    for j in range(NJ):
-        t = 23 + 7.7 * j
-        for dt, name, u in (
-            (0, "PB", 0), (0.1, "XF", 0), (0.2, "XD", 0), (0.3, "XF", 1),
-            (5.0, "X2", 0), (5.1, "XD", 1), (7.2, "X2", 1), (7.3, "BS", 0), (9.5, "X3", 0), (12, "X3", 1),
-            (12.1, "B2", 0), (16, "B3", 0), (17, "YF", 0), (19, "YF", 1),
-        ):
-            events.append((t + dt, name, j, u))
-    events.sort(key=lambda e: e[0])
-    return [e[1:] for e in events]
+    return [(step[:2], int(step[2]), int(step[3])) for step in ORDER]
 
 
 def kernel(v_hbm, w_hbm, c_hbm, mask, out, v, w, cc, core_s, core_r, own, zs, zr, ysum, ys, yr,
@@ -151,16 +150,23 @@
         lax.fori_loop(0, count // 256, tile, 0)
 
     width = out.shape[1]
-    tail = width - SPLIT
-    b_cols = pl.ds(SPLIT, tail)
+
+    def tail(j):
+        return width - SPLIT[j]
+
+    def b_cols(j):
+        return pl.ds(SPLIT[j], tail(j))
+
+    def yb_in(j):
+        return yb_r.at[j, :, :, :, pl.ds(0, tail(j))]
 
     def PB(j, u):
         arrived(sv.at[j, pl.ds(0, NZ)], one_r.at[j, 4])
         if j == 0:
             loads[2].wait()
-        product(j, SPLIT, tail)
+        product(j, SPLIT[j], tail(j))
         for k in (3, 2, 1):
-            send(pb.at[j, lax.rem(y + k, NY), :, :, b_cols], yb_r.at[j, k - 1],
+            send(pb.at[j, lax.rem(y + k, NY), :, :, b_cols(j)], yb_in(j).at[k - 1],
                  yb_ss.at[j], yb_rs.at[j], at_y(k))
 
     def halves(j, u):
@@ -221,32 +227,37 @@
             total = total + ya_r[j, k, :, cols].astype(F32)
         finish(j, lo, total)
 
-    b0, b1 = pl.ds(0, tail // 2), pl.ds(tail // 2, tail // 2)
+    def b_halves(j):
+        return pl.ds(0, tail(j) // 2), pl.ds(tail(j) // 2, tail(j) // 2)
 
     def BS(j, u):
-        arrived(yb_r.at[j], yb_rs.at[j])
-        total = pb[j, y, :, :, b_cols].astype(F32)
+        arrived(yb_in(j), yb_rs.at[j])
+        cols = pl.ds(0, tail(j))
+        total = pb[j, y, :, :, b_cols(j)].astype(F32)
         for k in range(3):
-            total = total + yb_r[j, k].astype(F32)
-        rb[j] = total
-        rb16[j] = total.astype(BF16)
+            total = total + yb_r[j, k, :, :, cols].astype(F32)
+        rb[j, :, :, cols] = total
+        rb16[j, :, :, cols] = total.astype(BF16)
+        b0, b1 = b_halves(j)
         send(rb16.at[j, xf, :, b0], bfar.at[j, :, b0], xb_s.at[j, 0], xb_r.at[j, 0], right)
         send(rb16.at[j, xf, :, b1], bfar.at[j, :, b1], xb_s.at[j, 1], xb_r.at[j, 1], left)
         send(rb16.at[j, xp, :, b1], bdir.at[j, :, b1], xb_s.at[j, 2], xb_r.at[j, 2], right)
         send(rb16.at[j, xm, :, b0], bdir.at[j, :, b0], xb_s.at[j, 3], xb_r.at[j, 3], left)
 
     def B2(j, u):
-        for i, (h, to, device) in enumerate(zip((b0, b1), (xp, xm), (right, left))):
+        for i, (h, to, device) in enumerate(zip(b_halves(j), (xp, xm), (right, left))):
             arrived(bfar.at[j, :, h], xb_r.at[j, i])
             bms[j, :, h] = (rb[j, to, :, h] + bfar[j, :, h].astype(F32)).astype(BF16)
             send(bms.at[j, :, h], bmr.at[j, :, h], xb_s.at[j, 4 + i], xb_r.at[j, 4 + i], device)
 
     def B3(j, u):
+        b0, b1 = b_halves(j)
         arrived(bdir.at[j, :, b1], xb_r.at[j, 2])
         arrived(bdir.at[j, :, b0], xb_r.at[j, 3])
         arrived(bmr.at[j, :, b0], xb_r.at[j, 4])
         arrived(bmr.at[j, :, b1], xb_r.at[j, 5])
-        finish(j, SPLIT, rb[j, x] + bdir[j].astype(F32) + bmr[j].astype(F32))
+        cols = pl.ds(0, tail(j))
+        finish(j, SPLIT[j], rb[j, x, :, cols] + bdir[j, :, cols].astype(F32) + bmr[j, :, cols].astype(F32))
 
     steps = dict(S1=S1, S2=S2, S3=S3, S4=S4, PB=PB, XF=XF, XD=XD, X2=X2, X3=X3, YF=YF, BS=BS, B2=B2, B3=B3)
     for name, j, u in schedule():
@@ -262,18 +273,18 @@
             for slot in range(6):
                 arrived(far_r.at[j, :, :, pl.ds(lo, w_u // 2)], xa_s.at[j, u, slot])
             arrived(ya_r.at[j, :, :, pl.ds(lo, w_u)], ya_ss.at[j, u])
-        arrived(yb_r.at[j], yb_ss.at[j])
+        arrived(yb_in(j), yb_ss.at[j])
         for slot in range(6):
-            arrived(bfar.at[j, :, b0], xb_s.at[j, slot])
+            arrived(bfar.at[j, :, b_halves(j)[0]], xb_s.at[j, slot])
 
 
 def local(valence_pairs, screened, conduction_pairs, window_mask):
     inner = screened.shape[1]
     width = conduction_pairs.shape[0]
-    tail = width - SPLIT
+    head, tail = max(SPLIT), width - min(SPLIT)
     vt = valence_pairs.T
     vmem, dma = pltpu.VMEM, pltpu.SemaphoreType.DMA
-    any_space = pl.BlockSpec(memory_space=pl.ANY)
+    any_space = pl.BlockSpec(memory_space=pltpu.HBM)
     nu = max(len(units) for units in UNITS)
     scratch = [
         vmem(vt.shape, BF16), vmem(screened.shape, BF16), vmem(conduction_pairs.shape, BF16),
@@ -283,9 +294,9 @@
         vmem((NJ, RW, inner), F32), vmem((NJ, RW, inner), BF16), vmem((NJ, RW, inner), BF16),
         vmem((NJ, 2 * NZ, RW, inner), BF16),
         vmem((NJ, NY, NX, RW, width), BF16),
-        vmem((NJ, NY, RW, SPLIT), BF16), vmem((NJ, NY, RW, SPLIT), BF16),
-        vmem((NJ, NY, RW, SPLIT), BF16), vmem((NJ, NY, RW, SPLIT), BF16),
-        vmem((NJ, NY - 1, RW, SPLIT), BF16), vmem((NJ, NY - 1, RW, SPLIT), BF16),
+        vmem((NJ, NY, RW, head), BF16), vmem((NJ, NY, RW, head), BF16),
+        vmem((NJ, NY, RW, head), BF16), vmem((NJ, NY, RW, head), BF16),
+        vmem((NJ, NY - 1, RW, head), BF16), vmem((NJ, NY - 1, RW, head), BF16),
         vmem((NJ, NY - 1, NX, RW, tail), BF16),
         vmem((NJ, NX, RW, tail), F32), vmem((NJ, NX, RW, tail), BF16),
         vmem((NJ, RW, tail), BF16), vmem((NJ, RW, tail), BF16),

time: 80.4 us -> 78.4 us (0.975)
  Pallas kernels: 78.5 us -> 76.5 us
    pallas_call x1, Pallas kernels: 78.5 us -> 76.5 us  [local(): pl.pallas_call(kernel, out_shape=jax.ShapeDtypeStruct((NJ * RW, width), B...]
where the time goes in v3:
time: 78.4 us; the launch traced here: 78.2 us
  Pallas kernels  76.5 us (98%)
  local copies, waits for them, and re-layouts  1.67 us (2%)
    pallas_call x1, Pallas kernels, local(): pl.pallas_call(kernel, out_shape=jax.ShapeDtypeStruct((NJ * RW, width), B...  76.5 us
    unnamed x1, local copies, waits for them, and re-layouts  1.67 us

profile of v3, /device:TPU:1, one launch (start us, length us, event | category | flops | bytes accessed | tf_op | source)
XLA Modules:
  0.0 78.2 jit_solution(6916323832771456755)
XLA Ops:
  0.0 76.5 %window.1 = bf16[64,2048]{1,0:T(8,128)(2,1)} custom-call(bf16[320,1024]{1,0:T(8,128)(2,1)} %bitcast.1, bf16[320,640]{1,0:T(8,128)(2,1)} %w_hbm.1, bf16[2048,640]{1,0:T(8,128)(2,1)} %c_hbm.1, s32[8,16]{1,0:T(8,128)} %mask.1), custom_call_target="tpu_custom_call" | custom-call | tf_op jit(solution)/shard_map/window/pallas_call | solution.py:308
  76.5 1.7 %copy.6 = bf16[64,2048]{1,0:T(8,128)(2,1)} copy(bf16[64,2048]{1,0:T(8,128)(2,1)} %window.1) | data formatting | bytes 524288

commit v4 on v3

--- a/solution.py
+++ b/solution.py
@@ -108,9 +108,14 @@
 
     def S1(j, u):
         arrived(core_r.at[j], one_r.at[j, 0])
-        total = own[j] + core_r[j].astype(F32)
-        own[j] = total
-        zs[j] = total.astype(BF16)
+
+        def add(i, carry):
+            total = own[j, i] + core_r[j, i].astype(F32)
+            own[j, i] = total
+            zs[j, i] = total.astype(BF16)
+            return carry
+
+        lax.fori_loop(0, NZ, add, 0)
         for k in HOPS:
             send(zs.at[j, lax.rem(z + k, NZ)], zr.at[j, k - 1],
                  one_s.at[j, 1], one_r.at[j, 1], at_z(k))
@@ -187,7 +192,14 @@
     def X2(j, u):
         for i, (h, to, device) in enumerate(zip(halves(j, u), (xp, xm), (right, left))):
             arrived(far_r.at[j, :, :, h], xa_r.at[j, u, i])
-            mrg_s[j, :, :, h] = (pb[j, :, to, :, h].astype(F32) + far_r[j, :, :, h].astype(F32)).astype(BF16)
+
+            def add(i, carry):
+                mrg_s[j, i, :, h] = (
+                    pb[j, i, to, :, h].astype(F32) + far_r[j, i, :, h].astype(F32)
+                ).astype(BF16)
+                return carry
+
+            lax.fori_loop(0, NY, add, 0)
             send(mrg_s.at[j, :, :, h], mrg_r.at[j, :, :, h], xa_s.at[j, u, 4 + i], xa_r.at[j, u, 4 + i], device)
 
     def X3(j, u):
@@ -197,12 +209,17 @@
         arrived(mrg_r.at[j, :, :, h0], xa_r.at[j, u, 4])
         arrived(mrg_r.at[j, :, :, h1], xa_r.at[j, u, 5])
         cols = pl.ds(*UNITS[j][u])
-        for k in (3, 2, 1):
-            yd = lax.rem(y + k, NY)
-            ya_s[j, k - 1, :, cols] = (
+
+        def add(i, carry):
+            yd = lax.rem(y + 1 + i, NY)
+            ya_s[j, i, :, cols] = (
                 pb[j, yd, x, :, cols].astype(F32) + dir_r[j, yd, :, cols].astype(F32)
                 + mrg_r[j, yd, :, cols].astype(F32)
             ).astype(BF16)
+            return carry
+
+        lax.fori_loop(0, NY - 1, add, 0)
+        for k in (3, 2, 1):
             send(ya_s.at[j, k - 1, :, cols], ya_r.at[j, k - 1, :, cols],
                  ya_ss.at[j, u], ya_rs.at[j, u], at_y(k))
 
@@ -219,13 +236,24 @@
         lo, w_u = UNITS[j][u]
         cols = pl.ds(lo, w_u)
         arrived(ya_r.at[j, :, :, cols], ya_rs.at[j, u])
-        total = (
-            pb[j, y, x, :, cols].astype(F32) + dir_r[j, y, :, cols].astype(F32)
-            + mrg_r[j, y, :, cols].astype(F32)
-        )
-        for k in range(3):
-            total = total + ya_r[j, k, :, cols].astype(F32)
-        finish(j, lo, total)
+
+        def add(i, carry):
+            at = pl.multiple_of(lo + i * 256, 256)
+            cols = pl.ds(at, 256)
+            total = (
+                pb[j, y, x, :, cols].astype(F32) + dir_r[j, y, :, cols].astype(F32)
+                + mrg_r[j, y, :, cols].astype(F32)
+            )
+            for k in range(3):
+                total = total + ya_r[j, k, :, cols].astype(F32)
+            for t in range(2):
+                live = mask[row_block, lo // 128 + 2 * i + t].astype(F32)
+                out[j * RW:(j + 1) * RW, pl.ds(pl.multiple_of(at + t * 128, 128), 128)] = (
+                    total[:, t * 128:(t + 1) * 128] * live
+                ).astype(BF16)
+            return carry
+
+        lax.fori_loop(0, w_u // 256, add, 0)
 
     def b_halves(j):
         return pl.ds(0, tail(j) // 2), pl.ds(tail(j) // 2, tail(j) // 2)
@@ -233,11 +261,16 @@
     def BS(j, u):
         arrived(yb_in(j), yb_rs.at[j])
         cols = pl.ds(0, tail(j))
-        total = pb[j, y, :, :, b_cols(j)].astype(F32)
-        for k in range(3):
-            total = total + yb_r[j, k, :, :, cols].astype(F32)
-        rb[j, :, :, cols] = total
-        rb16[j, :, :, cols] = total.astype(BF16)
+
+        def add(i, carry):
+            total = pb[j, y, i, :, b_cols(j)].astype(F32)
+            for k in range(3):
+                total = total + yb_r[j, k, i, :, cols].astype(F32)
+            rb[j, i, :, cols] = total
+            rb16[j, i, :, cols] = total.astype(BF16)
+            return carry
+
+        lax.fori_loop(0, NX, add, 0)
         b0, b1 = b_halves(j)
         send(rb16.at[j, xf, :, b0], bfar.at[j, :, b0], xb_s.at[j, 0], xb_r.at[j, 0], right)
         send(rb16.at[j, xf, :, b1], bfar.at[j, :, b1], xb_s.at[j, 1], xb_r.at[j, 1], left)
@@ -312,7 +345,7 @@
         out_specs=pl.BlockSpec(memory_space=pltpu.VMEM),
         scratch_shapes=scratch,
         compiler_params=pltpu.CompilerParams(
-            collective_id=0, has_side_effects=True, vmem_limit_bytes=56 * 1024 * 1024
+            collective_id=0, has_side_effects=True, vmem_limit_bytes=56200000
         ),
         name="window",
     )(vt, screened, conduction_pairs, window_mask)

time: 78.4 us -> 77.4 us (0.987)
    unnamed x1 -> x3, local copies, waits for them, and re-layouts: 1.67 us -> 1.39 us
where the time goes in v4:
time: 77.4 us; the launch traced here: 77.2 us
  Pallas kernels  75.8 us (98%)
  local copies, waits for them, and re-layouts  1.39 us (2%)
    pallas_call x1, Pallas kernels, local(): pl.pallas_call(kernel, out_shape=jax.ShapeDtypeStruct((NJ * RW, width), B...  75.8 us

profile of v4, /device:TPU:1, one launch (start us, length us, event | category | flops | bytes accessed | tf_op | source)
XLA Modules:
  0.0 77.2 jit_solution(3306275451191373586)
XLA Ops:
  0.0 0.0 copy-start
  0.0 0.7 copy-done
  0.7 75.8 %window.1 = bf16[64,2048]{1,0:T(8,128)(2,1)S(1)} custom-call(bf16[320,1024]{1,0:T(8,128)(2,1)} %bitcast.1, bf16[320,640]{1,0:T(8,128)(2,1)} %w_hbm.1, bf16[2048,640]{1,0:T(8,128)(2,1)} %c_hbm.1, s32[8,16]{1,0:T(8,128)S(1)} %copy-done), custom_call_target="tpu_custom_call" | custom-call | tf_op jit(solution)/shard_map/window/pallas_call | solution.py:341
  76.5 0.7 copy.6
Async XLA Ops:
  0.0 0.7 copy-start

commit v5 on v4

--- a/solution.py
+++ b/solution.py
@@ -24,7 +24,7 @@
 )
 SPLIT = tuple(sum(units[-1]) for units in UNITS)
 ORDER = (
-    "S100", "S120", "S110", "S200", "S220", "S300", "S210", "S320", "S130", "S400", "PB00", "XF01",
+    "S100", "S120", "S110", "S200", "S220", "S300", "S210", "S320", "S400", "S130", "PB00", "XF01",
     "XD01", "XF00", "S420", "S310", "XD00", "PB20", "XF20", "S230", "X200", "XD20", "XF21", "S410",
     "PB10", "X220", "X300", "XD21", "X201", "S330", "XF11", "XF10", "X221", "X320", "S430", "XD10",
     "XD11", "X301", "PB30", "XF30", "X211", "X321", "XF31", "X210", "XD30", "X230", "X311", "BS10",

time: 77.4 us -> 77.6 us (level)
  no operation moved by 1% of the time
where the time goes in v5:
time: 77.6 us; the launch traced here: 77.4 us
  Pallas kernels  76 us (98%)
  local copies, waits for them, and re-layouts  1.39 us (2%)
    pallas_call x1, Pallas kernels, local(): pl.pallas_call(kernel, out_shape=jax.ShapeDtypeStruct((NJ * RW, width), B...  76 us

profile of v5, /device:TPU:1, one launch (start us, length us, event | category | flops | bytes accessed | tf_op | source)
XLA Modules:
  0.0 77.4 jit_solution(2533020606312249906)
XLA Ops:
  0.0 0.0 copy-start
  0.0 0.7 copy-done
  0.7 76.0 %window.1 = bf16[64,2048]{1,0:T(8,128)(2,1)S(1)} custom-call(bf16[320,1024]{1,0:T(8,128)(2,1)} %bitcast.1, bf16[320,640]{1,0:T(8,128)(2,1)} %w_hbm.1, bf16[2048,640]{1,0:T(8,128)(2,1)} %c_hbm.1, s32[8,16]{1,0:T(8,128)S(1)} %copy-done), custom_call_target="tpu_custom_call" | custom-call | tf_op jit(solution)/shard_map/window/pallas_call | solution.py:341
  76.7 0.7 copy.6
Async XLA Ops:
  0.0 0.7 copy-start
